TPU v7x, 32 devices: a whole 2x2x4 slice. The times are simulated.
32 devices in a mesh: dp: 4 (over y, core), tm: 8 (over z, x).
Axes of the slice: x: 2, y: 2, z: 4, core: 2. Of those that a mesh axis runs over, the one named last changes fastest.
Arguments:
- features: bfloat16 [4, 16, 48, 48, 128], P('dp', 'tm'), may hold values from -6 to 6
- frame_counts: int32 [4, 6], P('dp'), may hold values from 1 to 8, 16 in all within a row
- conv1_weight: bfloat16 [3, 3, 3, 128, 128], replicated, may hold values from -0.109375 to 0.109375
- conv1_bias: float32 [128], replicated, may hold values from -3 to 3
- shrink_weight: bfloat16 [512, 128], replicated, may hold values from -0.25 to 0.25
- shrink_bias: float32 [128], replicated, may hold values from -3 to 3
- conv2_weight: bfloat16 [3, 3, 3, 128, 128], replicated, may hold values from -0.109375 to 0.109375
- conv2_bias: float32 [128], replicated, may hold values from -3 to 3
- embed_weight: bfloat16 [512, 1152], replicated, may hold values from -0.25 to 0.25
- embed_bias: float32 [1152], replicated, may hold values from -3 to 3
- bucket_table: float32 [8, 1152], replicated, may hold values from -5 to 5
- bucket_ids: int32 [4, 2304], P('dp', 'tm'), may hold values from 0 to 7
- dest_owner: int32 [4, 2304], P('dp', 'tm'), may hold values from 0 to 3, as said below
- dest_offset: int32 [4, 2304], P('dp', 'tm'), may hold values from 0 to 575, as said below
Outputs:
- packs: bfloat16 [4, 4608, 1152], P('dp', 'tm')
Inputs may be any that keep to these rules, and one draw needn't show every extreme that they name: `dest_owner`: among the 288 rows of one device (r // 288 fixed) each owner is named at most 144 times; for each index of tm one owner is named exactly 144 times by every device of dp. `dest_offset`: the rows that share an owner and a value of r // 288 have distinct offsets.
All inputs are finite; a program needn't handle non-finite values.
Results may differ from a plain program's by a relative error of at most 0.0056.
Values may be sent and summed in bfloat16 or wider, within the bound.
A program may use at most 128 MiB of HBM per device.

v0:
```python
import jax
import jax.numpy as jnp
from jax import lax
from jax.sharding import PartitionSpec as P


def from_behind(value, axis, steps):
    count = lax.axis_size(axis)
    initial, last = (max(0, -steps), min(count, count - steps))
    return lax.ppermute(value, axis, [(source, source + steps) for source in range(initial, last)])


def frame_masks(counts, first_frame, length):
    frames = first_frame + jnp.arange(length, dtype=jnp.int32)
    bounds = jnp.cumsum(counts)

    def segment(moments):
        return jnp.sum((moments[:, None] >= bounds[None, :]).astype(jnp.int32), axis=1)

    current = segment(frames)
    columns = []
    for distance in (2, 1):
        earlier = frames - distance
        columns.append(((earlier >= 0) & (segment(earlier) == current)).astype(jnp.float32))
    return jnp.stack(columns, axis=1)


def causal_conv(window, valid, kernel, conv_bias):
    outputs = valid.shape[0]
    side = window.shape[1]
    channels = window.shape[3]
    nothing = jnp.zeros((), window.dtype)
    oldest = jnp.where(valid[:, 0, None, None, None] > 0, window[0:outputs], nothing)
    middle = jnp.where(valid[:, 1, None, None, None] > 0, window[1 : outputs + 1], nothing)
    stacked = jnp.concatenate([oldest, middle, window[2 : outputs + 2]], axis=-1)
    padded = jnp.pad(stacked, ((0, 0), (1, 1), (1, 1), (0, 0)))
    taps_all = kernel.transpose(1, 2, 0, 3, 4).reshape(3, 3, 3 * channels, channels)
    total = jnp.zeros((outputs * side * side, channels), jnp.float32)
    for row_step in range(3):
        for col_step in range(3):
            piece = padded[:, row_step : row_step + side, col_step : col_step + side, :].reshape(
                -1, 3 * channels
            )
            total = total + jnp.dot(
                piece, taps_all[row_step, col_step], preferred_element_type=jnp.float32
            )
    return total.reshape(outputs, side, side, channels) + conv_bias


def fold_blocks(receptive_field):
    frame_total = receptive_field.shape[0]
    side = receptive_field.shape[1]
    channels = receptive_field.shape[3]
    blocks = receptive_field.reshape(frame_total, side // 2, 2, side // 2, 2, channels).transpose(
        0, 1, 3, 2, 4, 5
    )
    return blocks.reshape(frame_total, side // 2, side // 2, 4 * channels)


def residual_section(window, valid, kernel, conv_bias, inputs):
    return (
        inputs.astype(jnp.float32) + jax.nn.silu(causal_conv(window, valid, kernel, conv_bias))
    ).astype(jnp.bfloat16)


def spatial_shrink(receptive_field, shrink_weight, shrink_bias):
    folded = fold_blocks(receptive_field)
    shape_out = folded.shape[:3] + (shrink_weight.shape[1],)
    mixed = (
        jnp.dot(
            folded.reshape(-1, folded.shape[3]), shrink_weight, preferred_element_type=jnp.float32
        )
        + shrink_bias
    )
    return mixed.astype(jnp.bfloat16).reshape(shape_out)


def embed_rows(patches, buckets, embed_weight, embed_bias, bucket_table):
    selector = (
        buckets[:, None] == jnp.arange(bucket_table.shape[0], dtype=jnp.int32)[None, :]
    ).astype(jnp.float32)
    looked = jnp.dot(selector, bucket_table, precision=lax.Precision.HIGHEST)
    latent = (
        jnp.dot(patches, embed_weight, preferred_element_type=jnp.float32) + embed_bias + looked
    )
    return latent.astype(jnp.bfloat16)


def shards(
    features,
    frame_counts,
    conv1_weight,
    conv1_bias,
    shrink_weight,
    shrink_bias,
    conv2_weight,
    conv2_bias,
    embed_weight,
    embed_bias,
    bucket_table,
    bucket_ids,
    dest_owner,
    dest_offset,
):
    slab = features[0]
    per_device = slab.shape[0]
    start = lax.axis_index("tm") * per_device
    counts = frame_counts[0]
    prior = from_behind(features, "tm", 1)[0]
    own_valid = frame_masks(counts, start, per_device)
    window = jnp.concatenate([prior, slab], axis=0)
    section_first = residual_section(window, own_valid, conv1_weight, conv1_bias, slab)
    reduced_result = spatial_shrink(section_first, shrink_weight, shrink_bias)
    reduced_prior = from_behind(reduced_result, "tm", 1)
    window_two = jnp.concatenate([reduced_prior, reduced_result], axis=0)
    reduced_own = window_two[window_two.shape[0] - per_device :]
    section_two = residual_section(window_two, own_valid, conv2_weight, conv2_bias, reduced_own)
    patches = fold_blocks(section_two).reshape(-1, 4 * section_two.shape[3])
    owners = dest_owner[0]
    offsets = dest_offset[0]
    buckets = bucket_ids[0]
    row_total = owners.shape[0]
    owner_count = lax.axis_size("dp")
    capacity = 2 * row_total // owner_count
    pack_size = owner_count * capacity
    match_flags = (owners[:, None] == jnp.arange(owner_count, dtype=jnp.int32)[None, :]).astype(
        jnp.int32
    )
    position = jnp.sum((jnp.cumsum(match_flags, axis=0) - 1) * match_flags, axis=1)
    slot_index = owners * capacity + position
    send_offsets = (
        jnp.full((owner_count * capacity,), pack_size, jnp.int32).at[slot_index].set(offsets)
    )
    width = embed_weight.shape[1]
    send_patches = (
        jnp.zeros((owner_count * capacity, patches.shape[1]), jnp.bfloat16)
        .at[slot_index]
        .set(patches)
    )
    send_buckets = jnp.zeros((owner_count * capacity,), jnp.int32).at[slot_index].set(buckets)
    got_patches, got_buckets, arrived_offsets = (
        lax.all_to_all(send_patches, "dp", split_axis=0, concat_axis=0, tiled=True),
        lax.all_to_all(send_buckets, "dp", split_axis=0, concat_axis=0, tiled=True),
        lax.all_to_all(send_offsets, "dp", split_axis=0, concat_axis=0, tiled=True),
    )
    arrived = embed_rows(got_patches, got_buckets, embed_weight, embed_bias, bucket_table)
    packed = (
        jnp.zeros((pack_size, width), jnp.bfloat16).at[arrived_offsets].set(arrived, mode="drop")
    )
    return packed[None]


def solution(mesh):
    return jax.shard_map(
        shards,
        mesh=mesh,
        in_specs=(
            P("dp", "tm", None, None, None),
            P("dp", None),
            P(),
            P(),
            P(),
            P(),
            P(),
            P(),
            P(),
            P(),
            P(),
            P("dp", "tm"),
            P("dp", "tm"),
            P("dp", "tm"),
        ),
        out_specs=P("dp", "tm", None),
        check_vma=False,
    )
```

profile of v0, /device:TPU:0, one launch (start us, length us, event | category | flops | bytes accessed | tf_op | source)
XLA Modules:
  0.0 125.4 jit_solution(11836560773250618514)
XLA Ops:
  0.0 6.0 %collective-permute-start = (bf16[1,2,48,48,128]{4,3,2,1,0:T(8,128)(2,1)}, bf16[1,2,48,48,128]{4,3,2,1,0:T(8,128)(2,1)}, u32[]{:S(2)}, u32[]{:S(2)}) collective-permute-start(bf16[1,2,48,48,128]{4,3,2,1,0:T(8,128)(2,1)} %param.14), channel_id=1, source_target_pairs={{0,1},{1,2},{2,3},{3,4},{4,5},{5,6},{6,7},{8,9},{9,10},{10,11},{11... | collective-permute-start | bytes 3538952 | tf_op jit(solution)/shard_map/ppermute | solution.py:10
  6.0 1.2 copy.50
  7.2 0.8 reduce-window.20
  8.5 2.8 %convert.14 = f32[2,24,2,24,2,128]{5,4,3,2,1,0:T(2,128)} convert(bf16[2,24,2,24,2,128]{5,4,3,2,1,0:T(2,128)(2,1)S(1)} %bitcast.150) | non-fusion elementwise | flops 589824 | bytes 3538944
  11.3 1.2 reduce-window.18
  12.8 0.8 reduce-window.19
  13.5 17.0 %collective-permute-done = bf16[1,2,48,48,128]{4,3,2,1,0:T(8,128)(2,1)} collective-permute-done((bf16[1,2,48,48,128]{4,3,2,1,0:T(8,128)(2,1)}, bf16[1,2,48,48,128]{4,3,2,1,0:T(8,128)(2,1)}, u32[]{:S(2)}, u32[]{:S(2)}) %collective-permute-start) | collective-permute-done | bytes 1179680 | tf_op jit(solution)/shard_map/ppermute | solution.py:10
  30.5 1.2 fusion.20
  31.8 1.8 %broadcast_select_fusion = bf16[2,48,48,128]{3,2,1,0:T(8,128)(2,1)S(1)} fusion(pred[2]{0:T(512)(128)(4,1)S(1)} %get-tuple-element.26, bf16[1,2,48,48,128]{4,3,2,1,0:T(8,128)(2,1)} %collective-permute-done), kind=kLoop, calls=%fused_computation.60 | loop fusion | flops 589824 | bytes 2359298 | tf_op jit(solution)/shard_map/jit(_where)/select_n | solution.py:33
  33.6 4.0 %select_maximum_fusion = bf16[2,50,50,384]{3,2,1,0:T(8,128)(2,1)S(1)} fusion(bf16[2,48,48,128]{3,2,1,0:T(8,128)(2,1)S(1)} %bitcast.152, bf16[2,48,48,128]{3,2,1,0:T(8,128)(2,1)S(1)} %fusion.20, bf16[2,48,48,128]{3,2,1,0:T(8,128)(2,1)S(1)} %broadcast_select_fusion), kind=kLoop, calls=%fused_computation.19 | loop fusion | flops 36480000 | bytes 7378944 | tf_op jit(solution)/shard_map/concatenate | solution.py:35
  37.7 10.5 %fusion.53 = (bf16[2,48,48,384]{3,2,1,0:T(8,128)(2,1)S(1)}, bf16[2,48,48,384]{3,2,1,0:T(8,128)(2,1)}, bf16[2,48,48,384]{3,2,1,0:T(8,128)(2,1)}, bf16[2,48,48,384...) fusion(bf16[2,50,50,384]{3,2,1,0:T(8,128)(2,1)S(1)} %select_max, ...), kind=kLoop, calls=%fused_computation.134 | loop fusion | bytes 56623104 | tf_op jit(solution)/shard_map/slice | solution.py:41
  48.1 1.1 fusion.37
  49.2 0.9 copy-done.6
  50.1 1.1 convolution_add_fusion.7
  51.2 0.9 copy-done.5
  52.1 1.1 convolution_add_fusion.6
  53.2 0.9 copy-done.4
  54.1 1.1 convolution_add_fusion.5
  55.2 3.8 %bitcast_select_fusion = bf16[4608,128]{1,0:T(8,128)(2,1)S(1)} fusion(bf16[1,2,48,48,128]{4,3,2,1,0:T(8,128)(2,1)} %collective-permute-done, pred[4608]{0:T(1024)(128)(4,1)S(1)} %broadcast_in_dim.76), kind=kLoop, calls=%fused_computation.59 | loop fusion | flops 589824 | bytes 2363904 | tf_op jit(solution)/shard_map/jit(_where)/select_n | solution.py:33
  59.1 1.2 convolution_add_fusion.4
  60.2 0.8 copy-done.3
  61.1 1.2 convolution_add_fusion.3
  62.2 0.8 copy-done.2
  63.1 1.1 convolution_add_fusion.2
  64.2 0.9 copy-done.1
  65.1 1.1 convolution_add_fusion.1
  66.2 1.1 convolution_add_fusion
  67.3 0.5 copy-done.8
  67.8 0.6 fusion.21
  68.5 0.9 copy.53
  69.4 0.5 reshape_reshape.6
  69.9 1.4 %fusion.15 = bf16[1152,128]{1,0:T(8,128)(2,1)S(1)} fusion(bf16[1152,512]{1,0:T(8,128)(2,1)S(1)} %reshape_reshape.6, bf16[512,128]{1,0:T(8,128)(2,1)} %param.18, f32[128]{0:T(128)} %param.19), kind=kOutput, calls=%fused_computation.48 | convolution fusion | flops 151289856 | bytes 1606144 | tf_op jit(solution)/shard_map/dot_general | solution.py:70
  71.3 4.4 %collective-permute-start.1 = (bf16[2,24,24,128]{3,2,1,0:T(8,128)(2,1)S(1)}, bf16[2,24,24,128]{3,2,1,0:T(8,128)(2,1)S(1)}, u32[]{:S(2)}, u32[]{:S(2)}) collective-permute-start(bf16[2,24,24,128]{3,2,1,0:T(8,128)(2,1)S(1)} %bitcast.155), channel_id=1, source_target_pairs={{0,1},{1,2},{2,3},{3,4},{4,5},{5,6},{6,7},{8,9},{9,10},{10,11},{11... | collective-permute-start | bytes 884744 | tf_op jit(solution)/shard_map/ppermute | solution.py:10
  75.7 0.7 add_bitcast_fusion
  76.4 0.7 reduce.6
  77.1 0.7 fusion.45
  77.8 2.9 %scatter_custom_fusion.2 = s32[576]{0:T(1024)S(1)} fusion(s32[288]{0:T(512)S(1)} %fusion.45, s32[288]{0:T(512)S(1)} %reduce.6, s32[]{:T(128)} %constant.17.clone.1), kind=kCustom, calls=%fused_computation.113 | custom fusion | bytes 2308 | tf_op jit(solution)/shard_map/scatter | solution.py:140
  80.8 0.7 all_to_all.31
  81.4 3.2 %all-to-all-start.2 = ((s32[4,144,1]{1,2,0:T(1,128)}), s32[4,144,1]{1,2,0:T(1,128)S(1)}, u32[]{:S(2)}, u32[]{:S(2)}) async-start(s32[4,144,1]{1,2,0:T(1,128)} %all_to_all.31), calls=%async_computation.2 | async-start | bytes 8192 | tf_op jit(solution)/shard_map/all_to_all | solution.py:143
  84.7 1.2 copy.54
  85.9 0.7 reduce.3
  86.6 3.1 %scatter_custom_fusion = s32[576]{0:T(1024)S(1)} fusion(s32[288]{0:T(512)S(1)} %fusion.45, s32[288]{0:T(512)S(1)} %reduce.3, s32[]{:T(128)} %constant.14.clone.1), kind=kCustom, calls=%fused_computation.115 | custom fusion | bytes 2308 | tf_op jit(solution)/shard_map/scatter | solution.py:132
  89.8 0.7 all_to_all.30
  90.5 0.7 broadcast_select_fusion.1
  91.1 0.5 select_maximum_fusion.2
  91.7 0.9 fusion.54
  92.5 0.4 fusion.36
  92.9 0.4 convolution_add_fusion.17
  93.3 0.4 convolution_add_fusion.16
  93.7 0.4 convolution_add_fusion.15
  94.1 0.4 convolution_add_fusion.14
  94.5 0.4 convolution_add_fusion.13
  94.9 0.4 convolution_add_fusion.12
  95.3 0.4 convolution_add_fusion.11
  95.8 0.4 convolution_add_fusion.10
  96.2 3.3 %all-to-all-start = ((s32[4,144,1]{1,2,0:T(1,128)}), s32[4,144,1]{1,2,0:T(1,128)S(1)}, u32[]{:S(2)}, u32[]{:S(2)}) async-start(s32[4,144,1]{1,2,0:T(1,128)} %all_to_all.30), calls=%async_computation | async-start | bytes 8192 | tf_op jit(solution)/shard_map/all_to_all | solution.py:144
  99.4 0.7 fusion.34
  100.3 2.5 %scatter_custom_fusion.1 = bf16[576,512]{1,0:T(8,128)(2,1)} fusion(s32[288]{0:T(512)S(1)} %fusion.45, bf16[288,512]{1,0:T(8,128)(2,1)S(1)} %reshape.267, bf16[]{:T(256)} %constant.13.clone.1), kind=kCustom, calls=%fused_computation.76 | custom fusion | bytes 589826 | tf_op jit(solution)/shard_map/scatter | solution.py:138
  102.7 0.5 all-to-all-done
  103.2 3.5 %all-to-all-start.1 = ((bf16[4,144,512]{2,1,0:T(8,128)(2,1)}), bf16[4,144,512]{2,1,0:T(8,128)(2,1)S(1)}, u32[]{:S(2)}, u32[]{:S(2)}) async-start(bf16[4,144,512]{2,1,0:T(8,128)(2,1)} %bitcast.59), calls=%async_computation.1 | async-start | bytes 1179648 | tf_op jit(solution)/shard_map/all_to_all | solution.py:142
  107.0 9.3 %all-to-all-done.1 = bf16[4,144,512]{2,1,0:T(8,128)(2,1)S(1)} async-done(((bf16[4,144,512]{2,1,0:T(8,128)(2,1)}), bf16[4,144,512]{2,1,0:T(8,128)(2,1)S(1)}, u32[]{:S(2)}, u32[]{:S(2)}) %all-to-all-start.1) | async-done | bytes 589856 | tf_op jit(solution)/shard_map/all_to_all | solution.py:142
  116.2 0.9 convolution_add_fusion.9
  117.2 1.4 %fusion.11 = bf16[576,1152]{1,0:T(8,128)(2,1)S(1)} fusion(f32[576,1152]{1,0:T(8,128)S(1)} %convolution_add_fusion.9, f32[8,1152]{1,0:T(8,128)S(1)} %copy-done.11, s32[576]{0:T(1024)S(1)} %eq.60), kind=kOutput, calls=%fused_computation.35 | convolution fusion | flops 65032704 | bytes 4020480 | tf_op jit(solution)/shard_map/dot_general | solution.py:82
  118.6 6.9 %scatter_custom_fusion.3 = bf16[576,1152]{1,0:T(8,128)(2,1)} fusion(s32[576]{0:T(1024)S(1)} %fusion.40, bf16[576,1152]{1,0:T(8,128)(2,1)S(1)} %fusion.11, bf16[]{:T(256)} %constant.13.clone.1), kind=kCustom, calls=%fused_computation.67 | custom fusion | bytes 1327106 | tf_op jit(solution)/shard_map/scatter | solution.py:148
  (48 shorter events, 1.1 us)
Async XLA Ops:
  0.0 116.2 %copy-start = (bf16[512,1152]{1,0:T(8,128)(2,1)S(1)}, bf16[512,1152]{1,0:T(8,128)(2,1)}, u32[]{:S(2)}) copy-start(bf16[512,1152]{1,0:T(8,128)(2,1)} %param.22) | copy-start | bytes 3538948
  0.0 8.5 %copy-start.7 = (bf16[1,2,48,48,128]{4,3,2,1,0:T(8,128)(2,1)S(1)}, bf16[1,2,48,48,128]{4,3,2,1,0:T(8,128)(2,1)}, u32[]{:S(2)}) copy-start(bf16[1,2,48,48,128]{4,3,2,1,0:T(8,128)(2,1)} %param.14) | copy-start | bytes 3538948
  0.0 30.5 %collective-permute-start = (bf16[1,2,48,48,128]{4,3,2,1,0:T(8,128)(2,1)}, bf16[1,2,48,48,128]{4,3,2,1,0:T(8,128)(2,1)}, u32[]{:S(2)}, u32[]{:S(2)}) collective-permute-start(bf16[1,2,48,48,128]{4,3,2,1,0:T(8,128)(2,1)} %param.14), channel_id=1, source_target_pairs={{0,1},{1,2},{2,3},{3,4},{4,5},{5,6},{6,7},{8,9},{9,10},{10,11},{11... | collective-permute-start | bytes 3538952 | tf_op jit(solution)/shard_map/ppermute | solution.py:10
  6.0 5.3 %copy-start.12 = (s32[1,288]{1,0:T(1,128)S(1)}, s32[1,288]{1,0:T(1,128)}, u32[]{:S(2)}) copy-start(s32[1,288]{1,0:T(1,128)} %param.26) | copy-start | bytes 3460
  8.3 23.5 %copy-start.13 = (pred[2]{0:T(512)(128)(4,1)}, pred[2]{0:T(512)(128)(4,1)S(1)}, u32[]{:S(2)}) copy-start(pred[2]{0:T(512)(128)(4,1)S(1)} %get-tuple-element.27) | copy-start | bytes 10
  31.8 1.9 %copy-start.9 = (bf16[2,48,48,128]{3,2,1,0:T(8,128)(2,1)}, bf16[2,48,48,128]{3,2,1,0:T(8,128)(2,1)S(1)}, u32[]{:S(2)}) copy-start(bf16[2,48,48,128]{3,2,1,0:T(8,128)(2,1)S(1)} %fusion.20) | copy-start | bytes 3538948
  48.1 2.0 %copy-start.6 = (bf16[2,48,48,384]{3,2,1,0:T(8,128)(2,1)S(1)}, bf16[2,48,48,384]{3,2,1,0:T(8,128)(2,1)}, u32[]{:S(2)}) copy-start(bf16[2,48,48,384]{3,2,1,0:T(8,128)(2,1)} %get-tuple-element.14) | copy-start | bytes 10616836
  50.1 2.0 %copy-start.5 = (bf16[2,48,48,384]{3,2,1,0:T(8,128)(2,1)S(1)}, bf16[2,48,48,384]{3,2,1,0:T(8,128)(2,1)}, u32[]{:S(2)}) copy-start(bf16[2,48,48,384]{3,2,1,0:T(8,128)(2,1)} %get-tuple-element.13) | copy-start | bytes 10616836
  52.1 2.0 %copy-start.4 = (bf16[2,48,48,384]{3,2,1,0:T(8,128)(2,1)S(1)}, bf16[2,48,48,384]{3,2,1,0:T(8,128)(2,1)}, u32[]{:S(2)}) copy-start(bf16[2,48,48,384]{3,2,1,0:T(8,128)(2,1)} %get-tuple-element.12) | copy-start | bytes 10616836
  55.2 3.8 %copy-start.10 = (bf16[2,48,48,128]{3,2,1,0:T(8,128)(2,1)S(1)}, bf16[2,48,48,128]{3,2,1,0:T(8,128)(2,1)}, u32[]{:S(2)}) copy-start(bf16[2,48,48,128]{3,2,1,0:T(8,128)(2,1)} %copy-done.9) | copy-start | bytes 3538948
  59.1 2.0 %copy-start.3 = (bf16[2,48,48,384]{3,2,1,0:T(8,128)(2,1)S(1)}, bf16[2,48,48,384]{3,2,1,0:T(8,128)(2,1)}, u32[]{:S(2)}) copy-start(bf16[2,48,48,384]{3,2,1,0:T(8,128)(2,1)} %get-tuple-element.11) | copy-start | bytes 10616836
  61.1 2.0 %copy-start.2 = (bf16[2,48,48,384]{3,2,1,0:T(8,128)(2,1)S(1)}, bf16[2,48,48,384]{3,2,1,0:T(8,128)(2,1)}, u32[]{:S(2)}) copy-start(bf16[2,48,48,384]{3,2,1,0:T(8,128)(2,1)} %get-tuple-element.10) | copy-start | bytes 10616836
  63.1 2.0 %copy-start.1 = (bf16[2,48,48,384]{3,2,1,0:T(8,128)(2,1)S(1)}, bf16[2,48,48,384]{3,2,1,0:T(8,128)(2,1)}, u32[]{:S(2)}) copy-start(bf16[2,48,48,384]{3,2,1,0:T(8,128)(2,1)} %get-tuple-element.9) | copy-start | bytes 10616836
  66.2 1.7 %copy-start.8 = (f32[2,24,2,24,2,128]{5,4,3,2,1,0:T(2,128)S(1)}, f32[2,24,2,24,2,128]{5,4,3,2,1,0:T(2,128)}, u32[]{:S(2)}) copy-start(f32[2,24,2,24,2,128]{5,4,3,2,1,0:T(2,128)} %convert.14) | copy-start | bytes 7077892
  66.2 1.7 %copy-start.14 = (f32[128]{0:T(128)S(1)}, f32[128]{0:T(128)}, u32[]{:S(2)}) copy-start(f32[128]{0:T(128)} %param.17) | copy-start | bytes 1540
  71.3 19.2 %collective-permute-start.1 = (bf16[2,24,24,128]{3,2,1,0:T(8,128)(2,1)S(1)}, bf16[2,24,24,128]{3,2,1,0:T(8,128)(2,1)S(1)}, u32[]{:S(2)}, u32[]{:S(2)}) collective-permute-start(bf16[2,24,24,128]{3,2,1,0:T(8,128)(2,1)S(1)} %bitcast.155), channel_id=1, source_target_pairs={{0,1},{1,2},{2,3},{3,4},{4,5},{5,6},{6,7},{8,9},{9,10},{10,11},{11... | collective-permute-start | bytes 884744 | tf_op jit(solution)/shard_map/ppermute | solution.py:10
  81.4 14.7 %all-to-all-start.2 = ((s32[4,144,1]{1,2,0:T(1,128)}), s32[4,144,1]{1,2,0:T(1,128)S(1)}, u32[]{:S(2)}, u32[]{:S(2)}) async-start(s32[4,144,1]{1,2,0:T(1,128)} %all_to_all.31), calls=%async_computation.2 | async-start | bytes 8192 | tf_op jit(solution)/shard_map/all_to_all | solution.py:143
  95.3 4.1 %copy-start.15 = (f32[128]{0:T(128)S(1)}, f32[128]{0:T(128)}, u32[]{:S(2)}) copy-start(f32[128]{0:T(128)} %param.21) | copy-start | bytes 1540
  95.7 20.5 %copy-start.16 = (f32[1152]{0:T(1024)S(1)}, f32[1152]{0:T(1024)}, u32[]{:S(2)}) copy-start(f32[1152]{0:T(1024)} %param.23) | copy-start | bytes 13828
  96.2 7.1 %all-to-all-start = ((s32[4,144,1]{1,2,0:T(1,128)}), s32[4,144,1]{1,2,0:T(1,128)S(1)}, u32[]{:S(2)}, u32[]{:S(2)}) async-start(s32[4,144,1]{1,2,0:T(1,128)} %all_to_all.30), calls=%async_computation | async-start | bytes 8192 | tf_op jit(solution)/shard_map/all_to_all | solution.py:144
  103.2 13.0 %all-to-all-start.1 = ((bf16[4,144,512]{2,1,0:T(8,128)(2,1)}), bf16[4,144,512]{2,1,0:T(8,128)(2,1)S(1)}, u32[]{:S(2)}, u32[]{:S(2)}) async-start(bf16[4,144,512]{2,1,0:T(8,128)(2,1)} %bitcast.59), calls=%async_computation.1 | async-start | bytes 1179648 | tf_op jit(solution)/shard_map/all_to_all | solution.py:142
  116.2 0.9 copy-start.11
where the time goes:
time: 126 us; the launch traced here: 125 us
  local copies, waits for them, and re-layouts  38.5 us (31%)
  waiting for transfers between devices  26.8 us (21%)
  other arithmetic  22.2 us (18%)
  starting transfers between devices  20.4 us (16%)
  matrix products  17.2 us (14%)
    ppermute x2, waiting for transfers between devices, from_behind(): lax.ppermute(value, axis, [(source, source + steps) for source in range(i...  17 us
    dot_general x18, matrix products, causal_conv(): jnp.dot(piece, taps_all[row_step, col_step], preferred_element_type=jnp.f...  13.5 us
    slice x2, local copies, waits for them, and re-layouts, causal_conv(): padded[:, row_step:row_step + side, col_step:col_step + side, :]  11.3 us
    ppermute x2, starting transfers between devices, from_behind(): lax.ppermute(value, axis, [(source, source + steps) for source in range(i...  10.4 us
    all_to_all x1, waiting for transfers between devices, shards(): lax.all_to_all(send_patches, 'dp', split_axis=0, concat_axis=0, tiled=True)  9.27 us
    unnamed x37, local copies, waits for them, and re-layouts  8.32 us
    scatter x1, local copies, waits for them, and re-layouts, shards(): jnp.zeros((pack_size, width), jnp.bfloat16).at[arrived_offsets]  6.86 us
    select_n x3, other arithmetic, causal_conv(): jnp.where(valid[:, 0, None, None, None] > 0, window[0:outputs], nothing)  6.36 us
  transfers between devices with their start and end apart: 5, of which 3 were waited for; matrix products, arithmetic and copies ran while one was open for 21% of the time, Pallas kernels for 0%

commit v1 on v0

v1 whole, which is shorter than its diff:
```python
import functools
import jax
import jax.numpy as jnp
from jax import lax
from jax.experimental import pallas as pl
from jax.experimental.pallas import tpu as pltpu
from jax.sharding import PartitionSpec as P

MESH = pl.DeviceIdType.MESH
F32 = jnp.float32
BF16 = jnp.bfloat16
RED = ((0, 7), (7, 6), (13, 6), (19, 5))
FEAT = ((0, 15), (15, 12), (27, 12), (39, 9))
PIECES = 4
PAD = 8


def silu(v):
    return v / (1.0 + jnp.exp(-v))


def live_factors(counts_ref, first, videos):
    def segment(moment):
        total = jnp.int32(0)
        bound = jnp.int32(0)
        for i in range(videos):
            bound = bound + counts_ref[0, i]
            total = total + jnp.where(moment >= bound, 1, 0)
        return total

    seg = {d: segment(first + d) for d in (-2, -1, 0, 1)}

    def live(frame, distance):
        same = jnp.where(seg[frame] == seg[frame - distance], 1.0, 0.0)
        there = jnp.where(first + frame - distance >= 0, 1.0, 0.0)
        return (same * there).astype(F32)

    return live


def body(
    rows,
    pack,
    n_tm,
    n_dp,
    videos,
    feat,
    counts,
    w1,
    b1,
    sw,
    sb,
    w2,
    b2,
    bucket,
    owner,
    offset,
    patches_out,
    meta_out,
    xv,
    pv,
    p1,
    p2,
    wm1,
    wm2,
    acc,
    rsend,
    rrecv,
    fs,
    stage,
    psend,
    meta,
    local_sem,
    fsend_sem,
    frecv_sem,
    rsend_sem,
    rrecv_sem,
    psend_sem,
    precv_sem,
    msend_sem,
    mrecv_sem,
    own_sem,
):
    dp = lax.axis_index("dp")
    tm = lax.axis_index("tm")
    has_next = tm < n_tm - 1
    has_prev = tm > 0
    nxt = lax.rem(tm + 1, n_tm)
    prv = lax.rem(tm + n_tm - 1, n_tm)

    load = pltpu.make_async_copy(feat.at[0], xv, local_sem)
    load.start()

    barrier = pltpu.get_barrier_semaphore()

    @pl.when(has_next)
    def _():
        pl.semaphore_signal(barrier, inc=1, device_id=(dp, nxt), device_id_type=MESH)

    @pl.when(has_prev)
    def _():
        pl.semaphore_signal(barrier, inc=1, device_id=(dp, prv), device_id_type=MESH)

    for k in range(1, n_dp):
        pl.semaphore_signal(
            barrier, inc=1, device_id=(lax.rem(dp + k, n_dp), tm), device_id_type=MESH
        )

    beside = has_next.astype(jnp.int32) + has_prev.astype(jnp.int32)
    pl.semaphore_wait(barrier, n_dp - 1 + beside)

    def feat_copy(b):
        y0, n = FEAT[b]
        return pltpu.make_async_remote_copy(
            src_ref=feat.at[0, :, pl.ds(y0, n)],
            dst_ref=pv.at[:, pl.ds(y0, n)],
            send_sem=fsend_sem.at[b],
            recv_sem=frecv_sem.at[b],
            device_id=(dp, nxt),
            device_id_type=MESH,
        )

    def red_copy(b):
        n = 2 * RED[b][1] * 24
        return pltpu.make_async_remote_copy(
            src_ref=rsend.at[b, pl.ds(0, n)],
            dst_ref=rrecv.at[b, pl.ds(0, n)],
            send_sem=rsend_sem.at[b],
            recv_sem=rrecv_sem.at[b],
            device_id=(dp, nxt),
            device_id_type=MESH,
        )

    def patch_copy(b, k):
        return pltpu.make_async_remote_copy(
            src_ref=psend.at[b],
            dst_ref=patches_out.at[dp, b],
            send_sem=psend_sem.at[b, k],
            recv_sem=precv_sem.at[b, k],
            device_id=(lax.rem(dp + k, n_dp), tm),
            device_id_type=MESH,
        )

    def patch_own(b):
        return pltpu.make_async_copy(psend.at[b], patches_out.at[dp, b], own_sem.at[b])

    def meta_copy(k):
        return pltpu.make_async_remote_copy(
            src_ref=meta,
            dst_ref=meta_out.at[dp],
            send_sem=msend_sem.at[k],
            recv_sem=mrecv_sem.at[k],
            device_id=(lax.rem(dp + k, n_dp), tm),
            device_id_type=MESH,
        )

    def meta_own():
        return pltpu.make_async_copy(meta, meta_out.at[dp], own_sem.at[PIECES])

    @pl.when(has_next)
    def _():
        for b in range(PIECES):
            feat_copy(b).start()

    p1[...] = jnp.zeros(p1.shape, F32)
    p2[...] = jnp.zeros(p2.shape, F32)
    stage[...] = jnp.zeros(stage.shape, F32)

    @pl.when(tm == 0)
    def _():
        rrecv[...] = jnp.zeros(rrecv.shape, BF16)

    half = rows // 2
    quarter = half // PIECES
    width = meta.shape[1]
    block = width // PIECES
    row_at = lax.broadcasted_iota(jnp.int32, (rows, width), 0)
    col_at = lax.broadcasted_iota(jnp.int32, (rows, width), 1)
    order = jnp.zeros((rows, width), F32)
    for b in range(PIECES):
        for f in range(2):
            c0 = b * block + f * quarter
            hit = (
                (col_at - row_at == c0 - (f * half + b * quarter))
                & (col_at >= c0)
                & (col_at < c0 + quarter)
            )
            order = order + jnp.where(hit, 1.0, 0.0)
    code = (owner[...] * pack + offset[...] + 1).astype(F32)
    table = jnp.concatenate(
        [code, bucket[...].astype(F32), jnp.zeros((6, rows), F32)], axis=0
    )
    meta[...] = jnp.dot(
        table, order, precision=lax.Precision.HIGHEST, preferred_element_type=F32
    )
    meta_own().start()
    for k in range(1, n_dp):
        meta_copy(k).start()

    live = live_factors(counts, tm * 2, videos)
    for w, wm in ((w1, wm1), (w2, wm2)):
        wm[0, :, 0:128] = w[0] * live(0, 2).astype(BF16)
        wm[1, :, 0:128] = w[1] * live(0, 1).astype(BF16)
        wm[1, :, 128:256] = w[0] * live(1, 2).astype(BF16)
        wm[2, :, 0:128] = w[2]
        wm[2, :, 128:256] = w[1] * live(1, 1).astype(BF16)

    def field1(s, y0, n, parity):
        parts = []
        for dy in range(3):
            for dx in range(3):
                v = p1[s, y0 + dy : y0 + dy + n, pl.ds(PAD + parity + dx - 1, 24, stride=2), :]
                parts.append(v.reshape(n * 24, 128).astype(BF16))
        return jnp.concatenate(parts, axis=1)

    def field2(s, y0, n):
        parts = []
        for dy in range(3):
            for dx in range(3):
                v = p2[s, y0 + dy : y0 + dy + n, PAD + dx - 1 : PAD + dx + 23, :]
                parts.append(v.reshape(n * 24, 128).astype(BF16))
        return jnp.concatenate(parts, axis=1)

    def mm(a, w):
        return jnp.dot(a, w, preferred_element_type=F32)

    load.wait()
    for f in range(2):
        p1[2 + f, 1:49, PAD : PAD + 48, :] = xv[f].astype(F32)

    for b in range(PIECES):
        y0, n = 2 * RED[b][0], 2 * RED[b][1]
        for parity in range(2):
            both = mm(field1(2, y0, n, parity), wm1[2])
            last = mm(field1(3, y0, n, parity), w1[2])
            acc[0, parity, y0 * 24 : (y0 + n) * 24, :] = both[:, 0:128]
            acc[1, parity, y0 * 24 : (y0 + n) * 24, :] = both[:, 128:256] + last

    def section_one(b):
        f0, fn = FEAT[b]

        @pl.when(has_prev)
        def _():
            feat_copy(b).wait_recv()
            for f in range(2):
                p1[f, 1 + f0 : 1 + f0 + fn, PAD : PAD + 48, :] = pv[f, f0 : f0 + fn].astype(F32)

        y0, n = 2 * RED[b][0], 2 * RED[b][1]
        sides = []
        for parity in range(2):
            both = mm(field1(1, y0, n, parity), wm1[1])
            first = mm(field1(0, y0, n, parity), wm1[0, :, 0:128])
            outs = []
            for f in range(2):
                z = acc[f, parity, y0 * 24 : (y0 + n) * 24, :] + both[:, f * 128 : f * 128 + 128]
                if f == 0:
                    z = z + first
                z = z + b1[...]
                x = p1[2 + f, 1 + y0 : 1 + y0 + n, pl.ds(PAD + parity, 24, stride=2), :]
                outs.append((x.reshape(n * 24, 128) + silu(z)).reshape(n // 2, 2, 24, 128))
            sides.append(outs)
        pieces = []
        for by in range(2):
            for parity in range(2):
                pieces.append(
                    jnp.concatenate(
                        [sides[parity][f][:, by].reshape(n * 12, 128) for f in range(2)], axis=0
                    ).astype(BF16)
                )
        red = (mm(jnp.concatenate(pieces, axis=1), sw[...]) + sb[...]).astype(BF16)
        rsend[b, 0 : n * 24, :] = red

        @pl.when(has_next)
        def _():
            red_copy(b).start()

        wide = red.astype(F32).reshape(2, n // 2, 24, 128)
        for f in range(2):
            p2[2 + f, 1 + y0 // 2 : 1 + y0 // 2 + n // 2, PAD : PAD + 24, :] = wide[f]

    def section_two(b):
        r0, rn = RED[b]

        @pl.when(has_prev)
        def _():
            red_copy(b).wait_recv()

        wide = rrecv[b, 0 : 2 * rn * 24, :].astype(F32).reshape(2, rn, 24, 128)
        for f in range(2):
            p2[f, 1 + r0 : 1 + r0 + rn, PAD : PAD + 24, :] = wide[f]
        y0 = 6 * b
        both = mm(field2(1, y0, 6), wm2[1]) + mm(field2(2, y0, 6), wm2[2])
        ends = (mm(field2(0, y0, 6), wm2[0, :, 0:128]), mm(field2(3, y0, 6), w2[2]))
        for f in range(2):
            z = both[:, f * 128 : f * 128 + 128] + ends[f] + b2[...]
            x = p2[2 + f, 1 + y0 : 7 + y0, PAD : PAD + 24, :].reshape(144, 128)
            fs[f] = x + silu(z)
            for y in range(3):
                for by in range(2):
                    for bx in range(2):
                        lane = (by * 2 + bx) * 128
                        stage[f * 36 + y * 12 : f * 36 + y * 12 + 12, lane : lane + 128] = fs[
                            f, pl.ds(48 * y + 24 * by + bx, 12, stride=2), :
                        ]
        psend[b] = stage[...].astype(BF16)
        patch_own(b).start()
        for k in range(1, n_dp):
            patch_copy(b, k).start()

    for b in range(PIECES):
        section_one(b)
        if b > 0:
            section_two(b - 1)
    section_two(PIECES - 1)

    meta_own().wait()
    for k in range(1, n_dp):
        meta_copy(k).wait()
    for b in range(PIECES):
        patch_own(b).wait()
        for k in range(1, n_dp):
            patch_copy(b, k).wait()

    @pl.when(has_next)
    def _():
        for b in range(PIECES):
            feat_copy(b).wait_send()
            red_copy(b).wait_send()


def embed(n_dp, base, patches, meta, ew, eb, table, out):
    tile = out.shape[0]
    width = meta.shape[2]
    first = pl.program_id(0) * tile
    slot = lax.broadcasted_iota(jnp.int32, (tile, width), 0) + (first + base[0])
    slot = slot.astype(F32)
    bucket_at = lax.broadcasted_iota(jnp.int32, (128, width), 0)
    names = table.shape[0]
    name = lax.rem(bucket_at, names).astype(F32)
    inside = bucket_at < 3 * names
    got = jnp.zeros((tile, patches.shape[2]), F32)
    sel = jnp.zeros((tile, 128), F32)
    for d in range(n_dp):
        hot = jnp.where(slot == meta[d, 0:1, :], 1.0, 0.0).astype(BF16)
        named = jnp.where((name == meta[d, 1:2, :]) & inside, 1.0, 0.0).astype(BF16)
        got = got + jnp.dot(hot, patches[d], preferred_element_type=F32)
        sel = sel + lax.dot_general(
            hot, named, (((1,), (1,)), ((), ())), preferred_element_type=F32
        )
    full = table[...] + eb[...]
    high = full.astype(BF16).astype(F32)
    mid = (full - high).astype(BF16).astype(F32)
    low = full - high - mid
    split = jnp.concatenate(
        [high, mid, low, jnp.zeros((128 - 3 * names, full.shape[1]), F32)], axis=0
    ).astype(BF16)
    total = jnp.dot(got.astype(BF16), ew[...], preferred_element_type=F32)
    total = total + jnp.dot(sel.astype(BF16), split, preferred_element_type=F32)
    out[...] = total.astype(BF16)


def shards(
    n_dp,
    n_tm,
    features,
    frame_counts,
    conv1_weight,
    conv1_bias,
    shrink_weight,
    shrink_bias,
    conv2_weight,
    conv2_bias,
    embed_weight,
    embed_bias,
    bucket_table,
    bucket_ids,
    dest_owner,
    dest_offset,
):
    rows = dest_owner.shape[1]
    pack = 2 * rows
    lat = embed_weight.shape[1]
    block = 80
    wide = PIECES * block
    vmem = pl.BlockSpec(memory_space=pltpu.VMEM)
    anywhere = pl.BlockSpec(memory_space=pl.ANY)
    smem = pl.BlockSpec(memory_space=pltpu.SMEM)
    peers = max(n_dp, 2)
    dma = pltpu.SemaphoreType.DMA
    patches, meta = pl.pallas_call(
        functools.partial(body, rows, pack, n_tm, n_dp, frame_counts.shape[1]),
        out_shape=(
            jax.ShapeDtypeStruct((n_dp, PIECES, block, 512), BF16),
            jax.ShapeDtypeStruct((n_dp, 8, wide), F32),
        ),
        in_specs=[anywhere, smem] + [vmem] * 9,
        out_specs=(anywhere, anywhere),
        scratch_shapes=[
            pltpu.VMEM((2, 48, 48, 128), BF16),
            pltpu.VMEM((2, 48, 48, 128), BF16),
            pltpu.VMEM((4, 50, 48 + 2 * PAD, 128), F32),
            pltpu.VMEM((4, 26, 24 + 2 * PAD, 128), F32),
            pltpu.VMEM((3, 1152, 256), BF16),
            pltpu.VMEM((3, 1152, 256), BF16),
            pltpu.VMEM((2, 2, 48 * 24, 128), F32),
            pltpu.VMEM((PIECES, 336, 128), BF16),
            pltpu.VMEM((PIECES, 336, 128), BF16),
            pltpu.VMEM((2, 144, 128), F32),
            pltpu.VMEM((block, 512), F32),
            pltpu.VMEM((PIECES, block, 512), BF16),
            pltpu.VMEM((8, wide), F32),
            dma,
            dma((PIECES,)),
            dma((PIECES,)),
            dma((PIECES,)),
            dma((PIECES,)),
            dma((PIECES, peers)),
            dma((PIECES, peers)),
            dma((peers,)),
            dma((peers,)),
            dma((PIECES + 1,)),
        ],
        compiler_params=pltpu.CompilerParams(
            collective_id=0, has_side_effects=True, vmem_limit_bytes=56 * 1024 * 1024
        ),
        name="sections",
    )(
        features,
        frame_counts,
        conv1_weight.reshape(3, 1152, 128),
        conv1_bias.reshape(1, 128),
        shrink_weight,
        shrink_bias.reshape(1, 128),
        conv2_weight.reshape(3, 1152, 128),
        conv2_bias.reshape(1, 128),
        bucket_ids,
        dest_owner,
        dest_offset,
    )
    base = (lax.axis_index("dp") * pack + 1).astype(jnp.int32).reshape(1)
    tile = pack // 2
    packed = pl.pallas_call(
        functools.partial(embed, n_dp),
        grid=(pack // tile,),
        out_shape=jax.ShapeDtypeStruct((pack, lat), BF16),
        in_specs=[
            smem,
            pl.BlockSpec((n_dp, wide, 512), lambda i: (0, 0, 0)),
            pl.BlockSpec((n_dp, 8, wide), lambda i: (0, 0, 0)),
            pl.BlockSpec((512, lat), lambda i: (0, 0)),
            pl.BlockSpec((1, lat), lambda i: (0, 0)),
            pl.BlockSpec(bucket_table.shape, lambda i: (0, 0)),
        ],
        out_specs=pl.BlockSpec((tile, lat), lambda i: (i, 0)),
        compiler_params=pltpu.CompilerParams(vmem_limit_bytes=48 * 1024 * 1024),
        name="embed",
    )(
        base,
        patches.reshape(n_dp, wide, 512),
        meta,
        embed_weight,
        embed_bias.reshape(1, lat),
        bucket_table,
    )
    return packed[None]


def solution(mesh):
    sizes = dict(mesh.shape)
    return jax.shard_map(
        functools.partial(shards, sizes["dp"], sizes["tm"]),
        mesh=mesh,
        in_specs=(
            P("dp", "tm", None, None, None),
            P("dp", None),
            P(),
            P(),
            P(),
            P(),
            P(),
            P(),
            P(),
            P(),
            P(),
            P("dp", "tm"),
            P("dp", "tm"),
            P("dp", "tm"),
        ),
        out_specs=P("dp", "tm", None),
        check_vma=False,
    )
```

time: 126 us -> 56.6 us (0.45)
  the two profiles are of different devices: /device:TPU:0 before, /device:TPU:21 now
where the time goes in v1:
time: 56.6 us; the launch traced here: 56.3 us
  Pallas kernels  53.5 us (95%)
  local copies, waits for them, and re-layouts  2.81 us (5%)
    pallas_call x1, Pallas kernels, shards(): pl.pallas_call(functools.partial(body, rows, pack, n_tm, n_dp, frame_coun...  49.3 us
    pallas_call x1, Pallas kernels, shards(): pl.pallas_call(functools.partial(embed, n_dp), grid=(pack // tile,), out_...  4.17 us
    unnamed x8, local copies, waits for them, and re-layouts  2.11 us

profile of v1, /device:TPU:21, one launch (start us, length us, event | category | flops | bytes accessed | tf_op | source)
XLA Modules:
  0.0 56.3 jit_solution(15611782801515743039)
XLA Ops:
  0.0 0.7 %reshape.31.eb = f32[1,1152]{1,0:T(1,128)S(1)} reshape(f32[1152]{0:T(1024)} %param.23) | data formatting | bytes 9216 | tf_op jit(solution)/shard_map/reshape | solution.py:462
  0.7 0.0 copy-start.1
  0.7 0.0 copy-start.3
  0.7 49.3 %sections.1 = (bf16[4,4,80,512]{3,2,1,0:T(8,128)(2,1)}, f32[4,8,320]{2,1,0:T(8,128)}) custom-call(bf16[1,2,48,48,128]{4,3,2,1,0:T(8,128)(2,1)} %feat.1, s32[1,6]{1,0:T(1,128)} %counts.1, bf16[3,1152,128]{2,1,0:T(8,128)(2,1)} %bitcast.9, f32[1,128]{1,0:T(1,128)} %bitcast.11, bf16[512,128]{1,0:T(8,128)(2,1)} %sw.1, f32[1,128]{1,0:T(1,128)} %bitcast.12, ...), custom_call_target="tpu_custom_call" | custom-call | tf_op jit(solution)/shard_map/sections/pallas_call | solution.py:390
  50.0 0.0 copy-done.1
  50.0 0.0 copy-done.3
  50.0 0.0 copy-start
  50.0 1.3 %copy-done = bf16[4,4,80,512]{3,2,1,0:T(8,128)(2,1)S(1)} copy-done((bf16[4,4,80,512]{3,2,1,0:T(8,128)(2,1)S(1)}, bf16[4,4,80,512]{3,2,1,0:T(8,128)(2,1)}, u32[]{:S(2)}) %copy-start) | copy-done | bytes 1310744
  51.3 0.0 copy-start.2
  51.3 0.8 %copy-done.2 = f32[4,8,320]{2,1,0:T(8,128)S(1)} copy-done((f32[4,8,320]{2,1,0:T(8,128)S(1)}, f32[4,8,320]{2,1,0:T(8,128)}, u32[]{:S(2)}) %copy-start.2) | copy-done | bytes 40984
  52.1 4.2 %embed.1 = bf16[576,1152]{1,0:T(8,128)(2,1)} custom-call(s32[1]{0:T(128)} %bitcast.base, bf16[4,320,512]{2,1,0:T(8,128)(2,1)S(1)} %bitcast.8, f32[4,8,320]{2,1,0:T(8,128)S(1)} %copy-done.2, bf16[512,1152]{1,0:T(8,128)(2,1)S(1)} %copy-done.1, f32[1,1152]{1,0:T(1,128)S(1)} %reshape.31.eb, f32[8,1152]{1,0:T(8,128)S(1)} %copy-done.3), custom_call_target="tpu_custom_call" | custom-call | tf_op jit(solution)/shard_map/embed/pallas_call | solution.py:442
Async XLA Ops:
  0.7 49.3 %copy-start.1 = (bf16[512,1152]{1,0:T(8,128)(2,1)S(1)}, bf16[512,1152]{1,0:T(8,128)(2,1)}, u32[]{:S(2)}) copy-start(bf16[512,1152]{1,0:T(8,128)(2,1)} %ew.1) | copy-start | bytes 3538948
  0.7 49.3 %copy-start.3 = (f32[8,1152]{1,0:T(8,128)S(1)}, f32[8,1152]{1,0:T(8,128)}, u32[]{:S(2)}) copy-start(f32[8,1152]{1,0:T(8,128)} %table.1) | copy-start | bytes 110596
  50.0 1.3 %copy-start = (bf16[4,4,80,512]{3,2,1,0:T(8,128)(2,1)S(1)}, bf16[4,4,80,512]{3,2,1,0:T(8,128)(2,1)}, u32[]{:S(2)}) copy-start(bf16[4,4,80,512]{3,2,1,0:T(8,128)(2,1)} %get-tuple-element.7) | copy-start | bytes 3932164
  51.3 0.8 %copy-start.2 = (f32[4,8,320]{2,1,0:T(8,128)S(1)}, f32[4,8,320]{2,1,0:T(8,128)}, u32[]{:S(2)}) copy-start(f32[4,8,320]{2,1,0:T(8,128)} %get-tuple-element.8.meta) | copy-start | bytes 122884

commit v2 on v1

v2 whole, which is shorter than its diff:
```python
import functools
import jax
import jax.numpy as jnp
from jax import lax
from jax.experimental import pallas as pl
from jax.experimental.pallas import tpu as pltpu
from jax.sharding import PartitionSpec as P

MESH = pl.DeviceIdType.MESH
F32 = jnp.float32
BF16 = jnp.bfloat16
HALF = 27
FEAT = ((0, 9), (9, 9), (18, 9))
RED = ((0, 3), (3, 5), (8, 5))
PIECES = 3
PAD = 8


def silu(v):
    return v / (1.0 + jnp.exp(-v))


def live_factors(counts_ref, first, videos):
    def segment(moment):
        total = jnp.int32(0)
        bound = jnp.int32(0)
        for i in range(videos):
            bound = bound + counts_ref[0, i]
            total = total + jnp.where(moment >= bound, 1, 0)
        return total

    seg = {d: segment(first + d) for d in (-2, -1, 0, 1)}

    def live(frame, distance):
        same = jnp.where(seg[frame] == seg[frame - distance], 1.0, 0.0)
        there = jnp.where(first + frame - distance >= 0, 1.0, 0.0)
        return (same * there).astype(F32)

    return live


def body(
    rows,
    pack,
    n_tm,
    n_dp,
    videos,
    feat,
    counts,
    w1,
    b1,
    sw,
    sb,
    w2,
    b2,
    bucket,
    owner,
    offset,
    patches_out,
    meta_out,
    raw,
    p1,
    p2,
    wm1,
    wm2,
    rsend,
    rrecv,
    fs,
    stage,
    psend,
    pgot,
    meta,
    local_sem,
    xsend_sem,
    xrecv_sem,
    zsend_sem,
    zrecv_sem,
    rsend_sem,
    rrecv_sem,
    gsend_sem,
    grecv_sem,
    psend_sem,
    precv_sem,
    msend_sem,
    mrecv_sem,
    own_sem,
):
    dp = lax.axis_index("dp")
    tm = lax.axis_index("tm")
    side = lax.rem(tm, 2)
    mate = tm + 1 - 2 * side
    has_next = tm < n_tm - 2
    has_prev = tm > 1
    nxt = lax.rem(tm + 2, n_tm)
    prv = lax.rem(tm + n_tm - 2, n_tm)

    load = pltpu.make_async_copy(
        feat.at[0, :, pl.ds(21 * side, HALF)], raw.at[1 + side], local_sem
    )
    load.start()

    barrier = pltpu.get_barrier_semaphore()
    pl.semaphore_signal(barrier, inc=1, device_id=(dp, mate), device_id_type=MESH)

    @pl.when(has_next)
    def _():
        pl.semaphore_signal(barrier, inc=1, device_id=(dp, nxt), device_id_type=MESH)

    @pl.when(has_prev)
    def _():
        pl.semaphore_signal(barrier, inc=1, device_id=(dp, prv), device_id_type=MESH)

    for k in range(1, n_dp):
        pl.semaphore_signal(
            barrier, inc=1, device_id=(lax.rem(dp + k, n_dp), tm), device_id_type=MESH
        )
    beside = has_next.astype(jnp.int32) + has_prev.astype(jnp.int32)
    pl.semaphore_wait(barrier, n_dp + beside)

    def mate_copy(c):
        y0, n = FEAT[c]
        return pltpu.make_async_remote_copy(
            src_ref=feat.at[0, :, pl.ds(21 * (1 - side) + y0, n)],
            dst_ref=raw.at[1 + side, :, pl.ds(y0, n)],
            send_sem=xsend_sem.at[c],
            recv_sem=xrecv_sem.at[c],
            device_id=(dp, mate),
            device_id_type=MESH,
        )

    def next_copy(c):
        y0, n = FEAT[c]
        return pltpu.make_async_remote_copy(
            src_ref=raw.at[2, :, pl.ds(y0, n)],
            dst_ref=raw.at[0, :, pl.ds(y0, n)],
            send_sem=zsend_sem.at[c],
            recv_sem=zrecv_sem.at[c],
            device_id=(dp, nxt),
            device_id_type=MESH,
        )

    def red_copy(c):
        n = 2 * RED[c][1] * 24
        return pltpu.make_async_remote_copy(
            src_ref=rsend.at[c, pl.ds(0, n)],
            dst_ref=rrecv.at[c, pl.ds(0, n)],
            send_sem=rsend_sem.at[c],
            recv_sem=rrecv_sem.at[c],
            device_id=(dp, nxt),
            device_id_type=MESH,
        )

    def give_copy(e):
        return pltpu.make_async_remote_copy(
            src_ref=psend.at[e],
            dst_ref=pgot,
            send_sem=gsend_sem,
            recv_sem=grecv_sem,
            device_id=(dp, mate),
            device_id_type=MESH,
        )

    def patch_copy(src, half, lot, k):
        return pltpu.make_async_remote_copy(
            src_ref=src,
            dst_ref=patches_out.at[dp, half],
            send_sem=psend_sem.at[lot, k],
            recv_sem=precv_sem.at[lot, k],
            device_id=(lax.rem(dp + k, n_dp), tm),
            device_id_type=MESH,
        )

    def patch_own(src, half, lot):
        return pltpu.make_async_copy(src, patches_out.at[dp, half], own_sem.at[lot])

    def meta_copy(k):
        return pltpu.make_async_remote_copy(
            src_ref=meta,
            dst_ref=meta_out.at[dp],
            send_sem=msend_sem.at[k],
            recv_sem=mrecv_sem.at[k],
            device_id=(lax.rem(dp + k, n_dp), tm),
            device_id_type=MESH,
        )

    def meta_own():
        return pltpu.make_async_copy(meta, meta_out.at[dp], own_sem.at[2])

    for c in range(PIECES):
        mate_copy(c).start()
    load.wait()

    @pl.when(has_next & (side == 1))
    def _():
        for c in range(PIECES):
            next_copy(c).start()

    p1[...] = jnp.zeros(p1.shape, F32)
    p2[...] = jnp.zeros(p2.shape, F32)

    @pl.when(tm <= 1)
    def _():
        rrecv[...] = jnp.zeros(rrecv.shape, BF16)

    frame = rows // 2
    part = frame // 2
    row_at = lax.broadcasted_iota(jnp.int32, (rows, rows), 0)
    col_at = lax.broadcasted_iota(jnp.int32, (rows, rows), 1)
    order = jnp.zeros((rows, rows), F32)
    for b in range(2):
        for f in range(2):
            c0 = b * frame + f * part
            hit = (
                (col_at - row_at == c0 - (f * frame + b * part))
                & (col_at >= c0)
                & (col_at < c0 + part)
            )
            order = order + jnp.where(hit, 1.0, 0.0)
    code = (owner[...] * pack + offset[...] + 1).astype(F32)
    table = jnp.concatenate(
        [code, bucket[...].astype(F32), jnp.zeros((6, rows), F32)], axis=0
    )
    meta[...] = jnp.dot(
        table, order, precision=lax.Precision.HIGHEST, preferred_element_type=F32
    )
    meta_own().start()
    for k in range(1, n_dp):
        meta_copy(k).start()

    for e in range(2):
        live = live_factors(counts, (tm - side) * 2 + 2 * e, videos)
        for w, wm in ((w1, wm1), (w2, wm2)):
            wm[e, 0, :, 0:128] = w[0] * live(0, 2).astype(BF16)
            wm[e, 1, :, 0:128] = w[1] * live(0, 1).astype(BF16)
            wm[e, 1, :, 128:256] = w[0] * live(1, 2).astype(BF16)
            wm[e, 2, :, 0:128] = w[2]
            wm[e, 2, :, 128:256] = w[1] * live(1, 1).astype(BF16)

    def field1(s, y0, n, parity):
        parts = []
        for dy in range(3):
            for dx in range(3):
                v = p1[s, y0 + dy : y0 + dy + n, pl.ds(PAD + parity + dx - 1, 24, stride=2), :]
                parts.append(v.reshape(n * 24, 128).astype(BF16))
        return jnp.concatenate(parts, axis=1)

    def field2(s, n):
        parts = []
        for dy in range(3):
            for dx in range(3):
                v = p2[s, dy : dy + n, PAD + dx - 1 : PAD + dx + 23, :]
                parts.append(v.reshape(n * 24, 128).astype(BF16))
        return jnp.concatenate(parts, axis=1)

    def mm(a, w):
        return jnp.dot(a, w, preferred_element_type=F32)

    def widen(pair, y0, n):
        for f in range(2):
            p1[2 * pair + f, pl.ds(1 - side + y0, n), PAD : PAD + 48, :] = raw[
                pair, f, y0 : y0 + n
            ].astype(F32)

    widen(1 + side, 0, HALF)

    def section_one(e, c):
        f0, fn = FEAT[c]
        if e == 1:
            mate_copy(c).wait_recv()

            @pl.when(has_next & (side == 0))
            def _():
                next_copy(c).start()

            widen(2 - side, f0, fn)
        else:

            @pl.when(has_prev)
            def _():
                next_copy(c).wait_recv()
                widen(0, f0, fn)

        r0, rn = RED[c]
        y0, n = 2 * r0, 2 * rn
        sides = []
        for parity in range(2):
            both = mm(field1(2 * e + 1, y0, n, parity), wm1[e, 1])
            both = both + mm(field1(2 * e + 2, y0, n, parity), wm1[e, 2])
            ends = (
                mm(field1(2 * e, y0, n, parity), wm1[e, 0, :, 0:128]),
                mm(field1(2 * e + 3, y0, n, parity), w1[2]),
            )
            outs = []
            for f in range(2):
                z = both[:, f * 128 : f * 128 + 128] + ends[f] + b1[...]
                x = p1[2 + 2 * e + f, 1 + y0 : 1 + y0 + n, pl.ds(PAD + parity, 24, stride=2), :]
                outs.append((x.reshape(n * 24, 128) + silu(z)).reshape(rn, 2, 24, 128))
            sides.append(outs)
        pieces = []
        for by in range(2):
            for parity in range(2):
                pieces.append(
                    jnp.concatenate(
                        [sides[parity][f][:, by].reshape(rn * 24, 128) for f in range(2)], axis=0
                    ).astype(BF16)
                )
        red = (mm(jnp.concatenate(pieces, axis=1), sw[...]) + sb[...]).astype(BF16)
        if e == 1:
            rsend[c, 0 : 2 * rn * 24, :] = red

            @pl.when(has_next)
            def _():
                red_copy(c).start()

        wide = red.astype(F32).reshape(2, rn, 24, 128)
        for f in range(2):
            p2[2 + 2 * e + f, pl.ds(1 - side + r0, rn), PAD : PAD + 24, :] = wide[f]

    def section_two(e):
        if e == 0:

            @pl.when(has_prev)
            def _():
                for c in range(PIECES):
                    red_copy(c).wait_recv()

            for c in range(PIECES):
                r0, rn = RED[c]
                wide = rrecv[c, 0 : 2 * rn * 24, :].astype(F32).reshape(2, rn, 24, 128)
                for f in range(2):
                    p2[f, pl.ds(1 - side + r0, rn), PAD : PAD + 24, :] = wide[f]
        both = mm(field2(2 * e + 1, 12), wm2[e, 1]) + mm(field2(2 * e + 2, 12), wm2[e, 2])
        ends = (
            mm(field2(2 * e, 12), wm2[e, 0, :, 0:128]),
            mm(field2(2 * e + 3, 12), w2[2]),
        )
        for f in range(2):
            z = both[:, f * 128 : f * 128 + 128] + ends[f] + b2[...]
            x = p2[2 + 2 * e + f, 1:13, PAD : PAD + 24, :].reshape(288, 128)
            fs[f] = x + silu(z)
            for y in range(6):
                for by in range(2):
                    for bx in range(2):
                        lane = (by * 2 + bx) * 128
                        stage[f * 72 + y * 12 : f * 72 + y * 12 + 12, lane : lane + 128] = fs[
                            f, pl.ds(48 * y + 24 * by + bx, 12, stride=2), :
                        ]
        psend[e] = stage[...].astype(BF16)

        @pl.when(side == e)
        def _():
            patch_own(psend.at[e], side, 0).start()
            for k in range(1, n_dp):
                patch_copy(psend.at[e], side, 0, k).start()

        @pl.when(side != e)
        def _():
            give_copy(e).start()

    for e in (1, 0):
        for c in range(PIECES):
            section_one(e, c)
    section_two(1)
    section_two(0)

    give_copy(1 - side).wait_recv()
    patch_own(pgot, 1 - side, 1).start()
    for k in range(1, n_dp):
        patch_copy(pgot, 1 - side, 1, k).start()

    give_copy(1 - side).wait_send()
    meta_own().wait()
    for k in range(1, n_dp):
        meta_copy(k).wait()
    for c in range(PIECES):
        mate_copy(c).wait_send()

    @pl.when(has_next)
    def _():
        for c in range(PIECES):
            next_copy(c).wait_send()
            red_copy(c).wait_send()

    patch_own(psend.at[side], side, 0).wait()
    for k in range(1, n_dp):
        patch_copy(psend.at[side], side, 0, k).wait()
    patch_own(pgot, 1 - side, 1).wait()
    for k in range(1, n_dp):
        patch_copy(pgot, 1 - side, 1, k).wait()


def embed(n_dp, base, patches, meta, ew, eb, table, out):
    tile = out.shape[0]
    width = meta.shape[2]
    first = pl.program_id(0) * tile
    slot = lax.broadcasted_iota(jnp.int32, (tile, width), 0) + (first + base[0])
    slot = slot.astype(F32)
    bucket_at = lax.broadcasted_iota(jnp.int32, (128, width), 0)
    names = table.shape[0]
    name = lax.rem(bucket_at, names).astype(F32)
    inside = bucket_at < 3 * names
    got = jnp.zeros((tile, patches.shape[2]), F32)
    sel = jnp.zeros((tile, 128), F32)
    for d in range(n_dp):
        hot = jnp.where(slot == meta[d, 0:1, :], 1.0, 0.0).astype(BF16)
        named = jnp.where((name == meta[d, 1:2, :]) & inside, 1.0, 0.0).astype(BF16)
        got = got + jnp.dot(hot, patches[d], preferred_element_type=F32)
        sel = sel + lax.dot_general(
            hot, named, (((1,), (1,)), ((), ())), preferred_element_type=F32
        )
    full = table[...] + eb[...]
    high = full.astype(BF16).astype(F32)
    mid = (full - high).astype(BF16).astype(F32)
    low = full - high - mid
    split = jnp.concatenate(
        [high, mid, low, jnp.zeros((128 - 3 * names, full.shape[1]), F32)], axis=0
    ).astype(BF16)
    total = jnp.dot(got.astype(BF16), ew[...], preferred_element_type=F32)
    total = total + jnp.dot(sel.astype(BF16), split, preferred_element_type=F32)
    out[...] = total.astype(BF16)


def shards(
    n_dp,
    n_tm,
    features,
    frame_counts,
    conv1_weight,
    conv1_bias,
    shrink_weight,
    shrink_bias,
    conv2_weight,
    conv2_bias,
    embed_weight,
    embed_bias,
    bucket_table,
    bucket_ids,
    dest_owner,
    dest_offset,
):
    rows = dest_owner.shape[1]
    pack = 2 * rows
    lat = embed_weight.shape[1]
    block = rows // 2
    wide = rows
    vmem = pl.BlockSpec(memory_space=pltpu.VMEM)
    anywhere = pl.BlockSpec(memory_space=pl.ANY)
    smem = pl.BlockSpec(memory_space=pltpu.SMEM)
    peers = max(n_dp, 2)
    dma = pltpu.SemaphoreType.DMA
    patches, meta = pl.pallas_call(
        functools.partial(body, rows, pack, n_tm, n_dp, frame_counts.shape[1]),
        out_shape=(
            jax.ShapeDtypeStruct((n_dp, 2, block, 512), BF16),
            jax.ShapeDtypeStruct((n_dp, 8, wide), F32),
        ),
        in_specs=[anywhere, smem] + [vmem] * 9,
        out_specs=(anywhere, anywhere),
        scratch_shapes=[
            pltpu.VMEM((3, 2, HALF, 48, 128), BF16),
            pltpu.VMEM((6, HALF + 1, 48 + 2 * PAD, 128), F32),
            pltpu.VMEM((6, 14, 24 + 2 * PAD, 128), F32),
            pltpu.VMEM((2, 3, 1152, 256), BF16),
            pltpu.VMEM((2, 3, 1152, 256), BF16),
            pltpu.VMEM((PIECES, 240, 128), BF16),
            pltpu.VMEM((PIECES, 240, 128), BF16),
            pltpu.VMEM((2, 288, 128), F32),
            pltpu.VMEM((block, 512), F32),
            pltpu.VMEM((2, block, 512), BF16),
            pltpu.VMEM((block, 512), BF16),
            pltpu.VMEM((8, wide), F32),
            dma,
            dma((PIECES,)),
            dma((PIECES,)),
            dma((PIECES,)),
            dma((PIECES,)),
            dma((PIECES,)),
            dma((PIECES,)),
            dma,
            dma,
            dma((2, peers)),
            dma((2, peers)),
            dma((peers,)),
            dma((peers,)),
            dma((3,)),
        ],
        compiler_params=pltpu.CompilerParams(
            collective_id=0, has_side_effects=True, vmem_limit_bytes=56 * 1024 * 1024
        ),
        name="sections",
    )(
        features,
        frame_counts,
        conv1_weight.reshape(3, 1152, 128),
        conv1_bias.reshape(1, 128),
        shrink_weight,
        shrink_bias.reshape(1, 128),
        conv2_weight.reshape(3, 1152, 128),
        conv2_bias.reshape(1, 128),
        bucket_ids,
        dest_owner,
        dest_offset,
    )
    base = (lax.axis_index("dp") * pack + 1).astype(jnp.int32).reshape(1)
    tile = pack // 2
    packed = pl.pallas_call(
        functools.partial(embed, n_dp),
        grid=(pack // tile,),
        out_shape=jax.ShapeDtypeStruct((pack, lat), BF16),
        in_specs=[
            smem,
            pl.BlockSpec((n_dp, wide, 512), lambda i: (0, 0, 0)),
            pl.BlockSpec((n_dp, 8, wide), lambda i: (0, 0, 0)),
            pl.BlockSpec((512, lat), lambda i: (0, 0)),
            pl.BlockSpec((1, lat), lambda i: (0, 0)),
            pl.BlockSpec(bucket_table.shape, lambda i: (0, 0)),
        ],
        out_specs=pl.BlockSpec((tile, lat), lambda i: (i, 0)),
        compiler_params=pltpu.CompilerParams(vmem_limit_bytes=48 * 1024 * 1024),
        name="embed",
    )(
        base,
        patches.reshape(n_dp, wide, 512),
        meta,
        embed_weight,
        embed_bias.reshape(1, lat),
        bucket_table,
    )
    return packed[None]


def solution(mesh):
    sizes = dict(mesh.shape)
    return jax.shard_map(
        functools.partial(shards, sizes["dp"], sizes["tm"]),
        mesh=mesh,
        in_specs=(
            P("dp", "tm", None, None, None),
            P("dp", None),
            P(),
            P(),
            P(),
            P(),
            P(),
            P(),
            P(),
            P(),
            P(),
            P("dp", "tm"),
            P("dp", "tm"),
            P("dp", "tm"),
        ),
        out_specs=P("dp", "tm", None),
        check_vma=False,
    )
```

time: 56.6 us -> 52.8 us (0.933)
  Pallas kernels: 53.5 us -> 49.7 us
    pallas_call x1, Pallas kernels: 49.3 us -> 45.5 us  [shards(): pl.pallas_call(functools.partial(body, rows, pack, n_tm, n_dp, frame_coun...]
where the time goes in v2:
time: 52.8 us; the launch traced here: 52.5 us
  Pallas kernels  49.7 us (94%)
  local copies, waits for them, and re-layouts  2.77 us (5%)
    pallas_call x1, Pallas kernels, shards(): pl.pallas_call(functools.partial(body, rows, pack, n_tm, n_dp, frame_coun...  45.5 us
    pallas_call x1, Pallas kernels, shards(): pl.pallas_call(functools.partial(embed, n_dp), grid=(pack // tile,), out_...  4.15 us
    unnamed x8, local copies, waits for them, and re-layouts  2.07 us

profile of v2, /device:TPU:21, one launch (start us, length us, event | category | flops | bytes accessed | tf_op | source)
XLA Modules:
  0.0 52.5 jit_solution(10583933094844645069)
XLA Ops:
  0.0 0.7 %reshape.31.eb = f32[1,1152]{1,0:T(1,128)S(1)} reshape(f32[1152]{0:T(1024)} %param.23) | data formatting | bytes 9216 | tf_op jit(solution)/shard_map/reshape | solution.py:526
  0.7 0.0 copy-start
  0.7 0.0 copy-start.3
  0.7 45.5 %sections.1 = (bf16[4,2,144,512]{3,2,1,0:T(8,128)(2,1)}, f32[4,8,288]{2,1,0:T(8,128)}) custom-call(bf16[1,2,48,48,128]{4,3,2,1,0:T(8,128)(2,1)} %feat.1, s32[1,6]{1,0:T(1,128)} %counts.1, bf16[3,1152,128]{2,1,0:T(8,128)(2,1)} %bitcast.9, f32[1,128]{1,0:T(1,128)} %bitcast.11, bf16[512,128]{1,0:T(8,128)(2,1)} %sw.1, f32[1,128]{1,0:T(1,128)} %bitcast.12, ...), custom_call_target="tpu_custom_call" | custom-call | tf_op jit(solution)/shard_map/sections/pallas_call | solution.py:451
  46.3 0.0 copy-done
  46.3 0.0 copy-done.3
  46.3 0.0 copy-start.1
  46.3 1.3 %copy-done.1 = bf16[4,2,144,512]{3,2,1,0:T(8,128)(2,1)S(1)} copy-done((bf16[4,2,144,512]{3,2,1,0:T(8,128)(2,1)S(1)}, bf16[4,2,144,512]{3,2,1,0:T(8,128)(2,1)}, u32[]{:S(2)}) %copy-start.1) | copy-done | bytes 1179672
  47.5 0.0 copy-start.2
  47.6 0.8 %copy-done.2 = f32[4,8,288]{2,1,0:T(8,128)S(1)} copy-done((f32[4,8,288]{2,1,0:T(8,128)S(1)}, f32[4,8,288]{2,1,0:T(8,128)}, u32[]{:S(2)}) %copy-start.2) | copy-done | bytes 36888
  48.3 4.2 %embed.1 = bf16[576,1152]{1,0:T(8,128)(2,1)} custom-call(s32[1]{0:T(128)} %bitcast.base, bf16[4,288,512]{2,1,0:T(8,128)(2,1)S(1)} %bitcast.8, f32[4,8,288]{2,1,0:T(8,128)S(1)} %copy-done.2, bf16[512,1152]{1,0:T(8,128)(2,1)S(1)} %copy-done, f32[1,1152]{1,0:T(1,128)S(1)} %reshape.31.eb, f32[8,1152]{1,0:T(8,128)S(1)} %copy-done.3), custom_call_target="tpu_custom_call" | custom-call | tf_op jit(solution)/shard_map/embed/pallas_call | solution.py:506
Async XLA Ops:
  0.7 45.6 %copy-start = (bf16[512,1152]{1,0:T(8,128)(2,1)S(1)}, bf16[512,1152]{1,0:T(8,128)(2,1)}, u32[]{:S(2)}) copy-start(bf16[512,1152]{1,0:T(8,128)(2,1)} %ew.1) | copy-start | bytes 3538948
  0.7 45.6 %copy-start.3 = (f32[8,1152]{1,0:T(8,128)S(1)}, f32[8,1152]{1,0:T(8,128)}, u32[]{:S(2)}) copy-start(f32[8,1152]{1,0:T(8,128)} %table.1) | copy-start | bytes 110596
  46.3 1.3 %copy-start.1 = (bf16[4,2,144,512]{3,2,1,0:T(8,128)(2,1)S(1)}, bf16[4,2,144,512]{3,2,1,0:T(8,128)(2,1)}, u32[]{:S(2)}) copy-start(bf16[4,2,144,512]{3,2,1,0:T(8,128)(2,1)} %get-tuple-element.7) | copy-start | bytes 3538948
  47.5 0.8 %copy-start.2 = (f32[4,8,288]{2,1,0:T(8,128)S(1)}, f32[4,8,288]{2,1,0:T(8,128)}, u32[]{:S(2)}) copy-start(f32[4,8,288]{2,1,0:T(8,128)} %get-tuple-element.8.meta) | copy-start | bytes 110596

commit v3 on v2

--- a/solution.py
+++ b/solution.py
@@ -186,8 +186,7 @@
     def meta_own():
         return pltpu.make_async_copy(meta, meta_out.at[dp], own_sem.at[2])
 
-    for c in range(PIECES):
-        mate_copy(c).start()
+    mate_copy(0).start()
     load.wait()
 
     @pl.when(has_next & (side == 1))
@@ -266,6 +265,9 @@
     def section_one(e, c):
         f0, fn = FEAT[c]
         if e == 1:
+            mate_copy(c).wait_send()
+            if c + 1 < PIECES:
+                mate_copy(c + 1).start()
             mate_copy(c).wait_recv()
 
             @pl.when(has_next & (side == 0))
@@ -372,9 +374,6 @@
     meta_own().wait()
     for k in range(1, n_dp):
         meta_copy(k).wait()
-    for c in range(PIECES):
-        mate_copy(c).wait_send()
-
     @pl.when(has_next)
     def _():
         for c in range(PIECES):

time: 52.8 us -> 52.6 us (level)
  no operation moved by 1% of the time
where the time goes in v3:
time: 52.6 us; the launch traced here: 52.4 us
  Pallas kernels  49.6 us (94%)
  local copies, waits for them, and re-layouts  2.77 us (5%)
    pallas_call x1, Pallas kernels, shards(): pl.pallas_call(functools.partial(body, rows, pack, n_tm, n_dp, frame_coun...  45.4 us
    pallas_call x1, Pallas kernels, shards(): pl.pallas_call(functools.partial(embed, n_dp), grid=(pack // tile,), out_...  4.15 us
    unnamed x8, local copies, waits for them, and re-layouts  2.07 us

profile of v3, /device:TPU:21, one launch (start us, length us, event | category | flops | bytes accessed | tf_op | source)
XLA Modules:
  0.0 52.4 jit_solution(11768087031149440938)
XLA Ops:
  0.0 0.7 %reshape.31.eb = f32[1,1152]{1,0:T(1,128)S(1)} reshape(f32[1152]{0:T(1024)} %param.23) | data formatting | bytes 9216 | tf_op jit(solution)/shard_map/reshape | solution.py:525
  0.7 0.0 copy-start
  0.7 0.0 copy-start.3
  0.7 45.4 %sections.1 = (bf16[4,2,144,512]{3,2,1,0:T(8,128)(2,1)}, f32[4,8,288]{2,1,0:T(8,128)}) custom-call(bf16[1,2,48,48,128]{4,3,2,1,0:T(8,128)(2,1)} %feat.1, s32[1,6]{1,0:T(1,128)} %counts.1, bf16[3,1152,128]{2,1,0:T(8,128)(2,1)} %bitcast.9, f32[1,128]{1,0:T(1,128)} %bitcast.11, bf16[512,128]{1,0:T(8,128)(2,1)} %sw.1, f32[1,128]{1,0:T(1,128)} %bitcast.12, ...), custom_call_target="tpu_custom_call" | custom-call | tf_op jit(solution)/shard_map/sections/pallas_call | solution.py:450
  46.1 0.0 copy-done
  46.1 0.0 copy-done.3
  46.2 0.0 copy-start.1
  46.2 1.3 %copy-done.1 = bf16[4,2,144,512]{3,2,1,0:T(8,128)(2,1)S(1)} copy-done((bf16[4,2,144,512]{3,2,1,0:T(8,128)(2,1)S(1)}, bf16[4,2,144,512]{3,2,1,0:T(8,128)(2,1)}, u32[]{:S(2)}) %copy-start.1) | copy-done | bytes 1179672
  47.4 0.0 copy-start.2
  47.4 0.8 %copy-done.2 = f32[4,8,288]{2,1,0:T(8,128)S(1)} copy-done((f32[4,8,288]{2,1,0:T(8,128)S(1)}, f32[4,8,288]{2,1,0:T(8,128)}, u32[]{:S(2)}) %copy-start.2) | copy-done | bytes 36888
  48.2 4.2 %embed.1 = bf16[576,1152]{1,0:T(8,128)(2,1)} custom-call(s32[1]{0:T(128)} %bitcast.base, bf16[4,288,512]{2,1,0:T(8,128)(2,1)S(1)} %bitcast.8, f32[4,8,288]{2,1,0:T(8,128)S(1)} %copy-done.2, bf16[512,1152]{1,0:T(8,128)(2,1)S(1)} %copy-done, f32[1,1152]{1,0:T(1,128)S(1)} %reshape.31.eb, f32[8,1152]{1,0:T(8,128)S(1)} %copy-done.3), custom_call_target="tpu_custom_call" | custom-call | tf_op jit(solution)/shard_map/embed/pallas_call | solution.py:505
Async XLA Ops:
  0.7 45.4 %copy-start = (bf16[512,1152]{1,0:T(8,128)(2,1)S(1)}, bf16[512,1152]{1,0:T(8,128)(2,1)}, u32[]{:S(2)}) copy-start(bf16[512,1152]{1,0:T(8,128)(2,1)} %ew.1) | copy-start | bytes 3538948
  0.7 45.4 %copy-start.3 = (f32[8,1152]{1,0:T(8,128)S(1)}, f32[8,1152]{1,0:T(8,128)}, u32[]{:S(2)}) copy-start(f32[8,1152]{1,0:T(8,128)} %table.1) | copy-start | bytes 110596
  46.2 1.3 %copy-start.1 = (bf16[4,2,144,512]{3,2,1,0:T(8,128)(2,1)S(1)}, bf16[4,2,144,512]{3,2,1,0:T(8,128)(2,1)}, u32[]{:S(2)}) copy-start(bf16[4,2,144,512]{3,2,1,0:T(8,128)(2,1)} %get-tuple-element.7) | copy-start | bytes 3538948
  47.4 0.8 %copy-start.2 = (f32[4,8,288]{2,1,0:T(8,128)S(1)}, f32[4,8,288]{2,1,0:T(8,128)}, u32[]{:S(2)}) copy-start(f32[4,8,288]{2,1,0:T(8,128)} %get-tuple-element.8.meta) | copy-start | bytes 110596

commit v4 on v3

--- a/solution.py
+++ b/solution.py
@@ -93,6 +93,8 @@
     has_prev = tm > 1
     nxt = lax.rem(tm + 2, n_tm)
     prv = lax.rem(tm + n_tm - 2, n_tm)
+    twin = dp + 1 - 2 * lax.rem(dp, 2)
+    pairs = n_dp // 2
 
     load = pltpu.make_async_copy(
         feat.at[0, :, pl.ds(21 * side, HALF)], raw.at[1 + side], local_sem
@@ -166,7 +168,18 @@
             dst_ref=patches_out.at[dp, half],
             send_sem=psend_sem.at[lot, k],
             recv_sem=precv_sem.at[lot, k],
-            device_id=(lax.rem(dp + k, n_dp), tm),
+            device_id=(lax.rem(dp + 2 * k, n_dp) if k else twin, tm),
+            device_id_type=MESH,
+        )
+
+    def pass_copy(half, lot, k):
+        origin = lax.rem(dp + n_dp - 2 * k, n_dp)
+        return pltpu.make_async_remote_copy(
+            src_ref=patches_out.at[origin, half],
+            dst_ref=patches_out.at[origin, half],
+            send_sem=psend_sem.at[lot, pairs + k],
+            recv_sem=precv_sem.at[lot, pairs + k],
+            device_id=(twin, tm),
             device_id_type=MESH,
         )
 
@@ -352,7 +365,7 @@
         @pl.when(side == e)
         def _():
             patch_own(psend.at[e], side, 0).start()
-            for k in range(1, n_dp):
+            for k in range(pairs):
                 patch_copy(psend.at[e], side, 0, k).start()
 
         @pl.when(side != e)
@@ -367,8 +380,13 @@
 
     give_copy(1 - side).wait_recv()
     patch_own(pgot, 1 - side, 1).start()
-    for k in range(1, n_dp):
+    for k in range(pairs):
         patch_copy(pgot, 1 - side, 1, k).start()
+    lots = ((psend.at[side], side), (pgot, 1 - side))
+    for lot in range(2):
+        for k in range(1, pairs):
+            patch_copy(lots[lot][0], lots[lot][1], lot, k).wait_recv()
+            pass_copy(lots[lot][1], lot, k).start()
 
     give_copy(1 - side).wait_send()
     meta_own().wait()
@@ -380,12 +398,13 @@
             next_copy(c).wait_send()
             red_copy(c).wait_send()
 
-    patch_own(psend.at[side], side, 0).wait()
-    for k in range(1, n_dp):
-        patch_copy(psend.at[side], side, 0, k).wait()
-    patch_own(pgot, 1 - side, 1).wait()
-    for k in range(1, n_dp):
-        patch_copy(pgot, 1 - side, 1, k).wait()
+    for lot in range(2):
+        src, half = lots[lot]
+        patch_own(src, half, lot).wait()
+        patch_copy(src, half, lot, 0).wait()
+        for k in range(1, pairs):
+            patch_copy(src, half, lot, k).wait_send()
+            pass_copy(half, lot, k).wait()
 
 
 def embed(n_dp, base, patches, meta, ew, eb, table, out):

time: 52.6 us -> 48.3 us (0.918)
  Pallas kernels: 49.6 us -> 45.1 us
    pallas_call x1, Pallas kernels: 45.4 us -> 41 us  [shards(): pl.pallas_call(functools.partial(body, rows, pack, n_tm, n_dp, frame_coun...]
where the time goes in v4:
time: 48.3 us; the launch traced here: 47.9 us
  Pallas kernels  45.1 us (93%)
  local copies, waits for them, and re-layouts  2.77 us (6%)
    pallas_call x1, Pallas kernels, shards(): pl.pallas_call(functools.partial(body, rows, pack, n_tm, n_dp, frame_coun...  41 us
    pallas_call x1, Pallas kernels, shards(): pl.pallas_call(functools.partial(embed, n_dp), grid=(pack // tile,), out_...  4.15 us
    unnamed x8, local copies, waits for them, and re-layouts  2.07 us

profile of v4, /device:TPU:21, one launch (start us, length us, event | category | flops | bytes accessed | tf_op | source)
XLA Modules:
  0.0 47.9 jit_solution(9077934789687181499)
XLA Ops:
  0.0 0.7 %reshape.31.eb = f32[1,1152]{1,0:T(1,128)S(1)} reshape(f32[1152]{0:T(1024)} %param.23) | data formatting | bytes 9216 | tf_op jit(solution)/shard_map/reshape | solution.py:544
  0.7 0.0 copy-start
  0.7 0.0 copy-start.3
  0.7 41.0 %sections.1 = (bf16[4,2,144,512]{3,2,1,0:T(8,128)(2,1)}, f32[4,8,288]{2,1,0:T(8,128)}) custom-call(bf16[1,2,48,48,128]{4,3,2,1,0:T(8,128)(2,1)} %feat.1, s32[1,6]{1,0:T(1,128)} %counts.1, bf16[3,1152,128]{2,1,0:T(8,128)(2,1)} %bitcast.9, f32[1,128]{1,0:T(1,128)} %bitcast.11, bf16[512,128]{1,0:T(8,128)(2,1)} %sw.1, f32[1,128]{1,0:T(1,128)} %bitcast.12, ...), custom_call_target="tpu_custom_call" | custom-call | tf_op jit(solution)/shard_map/sections/pallas_call | solution.py:469
  41.7 0.0 copy-done
  41.7 0.0 copy-done.3
  41.7 0.0 copy-start.1
  41.7 1.3 %copy-done.1 = bf16[4,2,144,512]{3,2,1,0:T(8,128)(2,1)S(1)} copy-done((bf16[4,2,144,512]{3,2,1,0:T(8,128)(2,1)S(1)}, bf16[4,2,144,512]{3,2,1,0:T(8,128)(2,1)}, u32[]{:S(2)}) %copy-start.1) | copy-done | bytes 1179672
  43.0 0.0 copy-start.2
  43.0 0.8 %copy-done.2 = f32[4,8,288]{2,1,0:T(8,128)S(1)} copy-done((f32[4,8,288]{2,1,0:T(8,128)S(1)}, f32[4,8,288]{2,1,0:T(8,128)}, u32[]{:S(2)}) %copy-start.2) | copy-done | bytes 36888
  43.8 4.2 %embed.1 = bf16[576,1152]{1,0:T(8,128)(2,1)} custom-call(s32[1]{0:T(128)} %bitcast.base, bf16[4,288,512]{2,1,0:T(8,128)(2,1)S(1)} %bitcast.8, f32[4,8,288]{2,1,0:T(8,128)S(1)} %copy-done.2, bf16[512,1152]{1,0:T(8,128)(2,1)S(1)} %copy-done, f32[1,1152]{1,0:T(1,128)S(1)} %reshape.31.eb, f32[8,1152]{1,0:T(8,128)S(1)} %copy-done.3), custom_call_target="tpu_custom_call" | custom-call | tf_op jit(solution)/shard_map/embed/pallas_call | solution.py:524
Async XLA Ops:
  0.7 41.0 %copy-start = (bf16[512,1152]{1,0:T(8,128)(2,1)S(1)}, bf16[512,1152]{1,0:T(8,128)(2,1)}, u32[]{:S(2)}) copy-start(bf16[512,1152]{1,0:T(8,128)(2,1)} %ew.1) | copy-start | bytes 3538948
  0.7 41.0 %copy-start.3 = (f32[8,1152]{1,0:T(8,128)S(1)}, f32[8,1152]{1,0:T(8,128)}, u32[]{:S(2)}) copy-start(f32[8,1152]{1,0:T(8,128)} %table.1) | copy-start | bytes 110596
  41.7 1.3 %copy-start.1 = (bf16[4,2,144,512]{3,2,1,0:T(8,128)(2,1)S(1)}, bf16[4,2,144,512]{3,2,1,0:T(8,128)(2,1)}, u32[]{:S(2)}) copy-start(bf16[4,2,144,512]{3,2,1,0:T(8,128)(2,1)} %get-tuple-element.7) | copy-start | bytes 3538948
  43.0 0.8 %copy-start.2 = (f32[4,8,288]{2,1,0:T(8,128)S(1)}, f32[4,8,288]{2,1,0:T(8,128)}, u32[]{:S(2)}) copy-start(f32[4,8,288]{2,1,0:T(8,128)} %get-tuple-element.8.meta) | copy-start | bytes 110596
